TPU v7x, 32 devices: a whole 2x2x4 slice. The times are simulated.
32 devices in a mesh: wide: 8 (over y, x, core), narrow: 4 (over z).
Axes of the slice: x: 2, y: 2, z: 4, core: 2. Of those that a mesh axis runs over, the one named last changes fastest.
Arguments:
- cache: bfloat16 [8, 8192, 128], P('wide', 'narrow'), may hold values from -6 to 6
- lookup_slots: int32 [8, 4096, 16], P('wide'), may hold values from 0 to 8191
- bag_lengths: int32 [8, 4096], P('wide'), may hold values from 1 to 16
- miss_rows: bfloat16 [8, 4096, 128], P('wide', 'narrow'), may hold values from -6 to 6
- miss_slots: int32 [8, 4096], P('wide', 'narrow'), may hold values from 0 to 8191, as said below
- holder_counts: int32 [8, 16], P('wide', 'narrow'), may hold values from 0 to 512, as said below
- w_first: bfloat16 [1024, 4096], P(None, 'narrow'), may hold values from -0.1875 to 0.1875
- b_first: float32 [4096], P('narrow'), may hold values from -4 to 4
- w_second: bfloat16 [4096, 4096], P('narrow'), may hold values from -0.09375 to 0.09375
- b_second: float32 [4096], P('narrow'), may hold values from -4 to 4
- w_out: bfloat16 [4096], P('narrow'), may hold values from -0.09375 to 0.09375
Outputs:
- top_hidden: bfloat16 [4096, 4096], P('wide', 'narrow')
- logits: float32 [4096], P('wide')
- cache_next: bfloat16 [8, 8192, 128], P('wide', 'narrow')
Inputs may be any that keep to these rules, and one draw needn't show every extreme that they name: `holder_counts`: entry h * 4 + o is the number of row blocks that holder h sections for owner o, the device holding slots o * 2048 to (o + 1) * 2048 - 1; a holder's counts sum to at most 1024, and this is reached by some holder of every table; the largest count, 512, is reached in every table. `miss_slots`: A holder's live entries are packed by owner, owner 0 first, as its counts say; each live entry names a slot of its owner, no slot twice in a table; entries past a holder's live ones are 0 and unused.
All inputs are finite; a program needn't handle non-finite values.
Results may differ from a plain program's by a relative error of at most 0.0076.
Values may be sent and summed in bfloat16 or wider, within the bound.
No kernel may reach another device: no remote copies, remote signals or barrier semaphores. Data moves between devices by JAX's collectives and lax.ppermute only.
A program may use at most 128 MiB of HBM per device.

v0:
```python
import math
import jax
import jax.numpy as jnp
from jax import lax
from jax.sharding import PartitionSpec as P

SEND_CAP = 512


def pool_rows(cache_table, lookups, lengths, owner_index):
    slot_count = cache_table.shape[0]
    emb_width = cache_table.shape[1]
    batch_rows, bag_size = lookups.shape
    local_slots = lookups - owner_index * slot_count
    usable = jnp.arange(bag_size, dtype=jnp.int32)[None, :] < lengths[:, None]
    usable = usable & (local_slots >= 0) & (local_slots < slot_count)
    safe_slots = jnp.clip(local_slots, 0, slot_count - 1)
    block_rows = math.gcd(batch_rows, 2048)
    block_count = batch_rows // block_rows

    def pool_block(member):
        positions, keep = member
        gathered = jnp.take(cache_table, positions, axis=0).astype(jnp.float32)
        return jnp.sum(jnp.where(keep[..., None], gathered, jnp.zeros((), jnp.float32)), axis=1)

    pooled = lax.map(
        pool_block,
        (
            safe_slots.reshape(block_count, block_rows, bag_size),
            usable.reshape(block_count, block_rows, bag_size),
        ),
    )
    return pooled.reshape(batch_rows, emb_width)


def body(
    cache,
    lookup_slots,
    bag_lengths,
    miss_rows,
    miss_slots,
    holder_counts,
    w_first,
    b_first,
    w_second,
    b_second,
    w_out,
):
    wide_count = lax.axis_size("wide")
    narrow_count = lax.axis_size("narrow")
    owner_index = lax.axis_index("narrow")
    cache_table = cache[0]
    slot_count = cache_table.shape[0]
    emb_width = cache_table.shape[1]
    lookups = lookup_slots[0]
    lengths = bag_lengths[0]
    batch_rows, bag_size = lookups.shape
    owner_rows = batch_rows // wide_count
    quarter_rows = owner_rows // narrow_count
    whole_table = lax.all_gather(cache_table, "narrow", axis=0, tiled=True)
    own_lookups = lax.dynamic_index_in_dim(
        lookups.reshape(wide_count, narrow_count, quarter_rows, bag_size),
        owner_index,
        1,
        keepdims=False,
    )
    own_lengths = lax.dynamic_index_in_dim(
        lengths.reshape(wide_count, narrow_count, quarter_rows), owner_index, 1, keepdims=False
    )
    own_pooled = pool_rows(
        whole_table,
        own_lookups.reshape(wide_count * quarter_rows, bag_size),
        own_lengths.reshape(wide_count * quarter_rows),
        0,
    )
    summed = own_pooled.reshape(1, wide_count, quarter_rows, emb_width).astype(jnp.bfloat16)
    arrived = lax.all_to_all(summed, "wide", split_axis=1, concat_axis=0, tiled=True)
    arrived = arrived.reshape(wide_count, quarter_rows, emb_width)
    pooled = lax.all_gather(arrived, "narrow", axis=1, tiled=True)
    first_slab = w_first.reshape(wide_count, emb_width, w_first.shape[1])
    first_terms = jnp.einsum("fbe,feh->bh", pooled, first_slab, preferred_element_type=jnp.float32)
    first_hidden = jnp.maximum(first_terms + b_first, 0.0).astype(jnp.bfloat16)
    second_terms = jnp.dot(first_hidden, w_second, preferred_element_type=jnp.float32)
    second_summed = lax.psum_scatter(second_terms, "narrow", scatter_dimension=1, tiled=True)
    top_hidden = jnp.maximum(second_summed + b_second, 0.0).astype(jnp.bfloat16)
    logit_terms = jnp.dot(top_hidden, w_out, preferred_element_type=jnp.float32)
    logits = lax.psum(logit_terms, "narrow")
    sectioned = miss_rows[0]
    sectioned_slots = miss_slots[0]
    sectioned_counts = holder_counts[0]
    hold_rows = sectioned.shape[0]
    send_cap = SEND_CAP
    starts = jnp.cumsum(sectioned_counts) - sectioned_counts
    column_ids = jnp.arange(send_cap, dtype=jnp.int32)
    live = column_ids[None, :] < sectioned_counts[:, None]
    sources = jnp.where(live, starts[:, None] + column_ids[None, :], -1).reshape(
        narrow_count * send_cap
    )
    selector = (sources[:, None] == jnp.arange(hold_rows, dtype=jnp.int32)[None, :]).astype(
        jnp.bfloat16
    )
    slab_rows = jnp.dot(selector, sectioned, preferred_element_type=jnp.float32).astype(
        jnp.bfloat16
    )
    slab_rows = slab_rows.reshape(narrow_count, send_cap, emb_width)
    slab_slots = jnp.where(
        sources >= 0, jnp.take(sectioned_slots, jnp.maximum(sources, 0), axis=0), -1
    )
    slab_slots = slab_slots.reshape(narrow_count, send_cap)
    got_rows, got_slots = (
        lax.all_to_all(slab_rows, "narrow", split_axis=0, concat_axis=0, tiled=True),
        lax.all_to_all(slab_slots, "narrow", split_axis=0, concat_axis=0, tiled=True),
    )
    arrived_rows = got_rows.reshape(narrow_count * send_cap, emb_width)
    arrived_slots = got_slots.reshape(narrow_count * send_cap)
    targets = arrived_slots - owner_index * slot_count
    kept = (arrived_slots >= 0) & (targets >= 0) & (targets < slot_count)
    targets = jnp.where(kept, targets, -1)
    placing = (targets[:, None] == jnp.arange(slot_count, dtype=jnp.int32)[None, :]).astype(
        jnp.bfloat16
    )
    placed = jnp.einsum("as,ae->se", placing, arrived_rows, preferred_element_type=jnp.float32)
    struck = jnp.sum(placing.astype(jnp.float32), axis=0) > 0.5
    cache_next = jnp.where(struck[:, None], placed.astype(jnp.bfloat16), cache_table)[None]
    return (top_hidden, logits, cache_next)


def solution(mesh):
    return jax.shard_map(
        body,
        mesh=mesh,
        in_specs=(
            P("wide", "narrow", None),
            P("wide", None, None),
            P("wide", None),
            P("wide", "narrow", None),
            P("wide", "narrow"),
            P("wide", "narrow"),
            P(None, "narrow"),
            P("narrow"),
            P("narrow", None),
            P("narrow"),
            P("narrow"),
        ),
        out_specs=(P("wide", "narrow"), P("wide"), P("wide", "narrow", None)),
        check_vma=False,
    )
```

profile of v0, /device:TPU:0, one launch (start us, length us, event | category | flops | bytes accessed | tf_op | source)
XLA Modules:
  0.0 345.0 jit_solution(8075441370404629953)
XLA Ops:
  7.2 0.0 copy-start
  7.2 0.0 all-gather.5.cloned.1.call-start
  7.2 0.7 all-gather.5.cloned.1.call-update
  7.9 0.0 all-gather.7.cloned.1.call-start
  8.0 1.1 reshape_squeeze.7
  9.1 0.7 constant_dynamic-slice_fusion.1
  9.8 0.1 constant_dynamic-slice_fusion
  10.0 0.3 copy.29
  10.3 0.2 copy.31
  10.5 0.1 compare_select_fusion
  10.5 0.2 reshape.345
  10.8 0.3 copy.30
  11.0 46.9 %all-gather.5.cloned.1.call-done = bf16[1,8192,128]{2,1,0:T(8,128)(2,1)} async-done(((bf16[1,2048,128]{2,1,0:T(8,128)(2,1)}), bf16[1,8192,128]{2,1,0:T(8,128)(2,1)}) %all-gather.5.cloned.1.call-update) | async-done | bytes 2097168 | tf_op jit(solution)/shard_map/all_gather | solution.py:60
  58.0 57.2 %gather_fusion = bf16[16384,128]{1,0:T(8,128)(2,1)} fusion(bf16[8192,128]{1,0:T(8,128)(2,1)} %bitcast.81, s32[16384]{0:T(1024)S(1)} %broadcast_clamp_fusion), kind=kCustom, calls=%fused_computation | custom fusion | bytes 8454144 | tf_op jit(solution)/shard_map/while/body/eval_jaxpr/jit(_take)/gather | solution.py:23
  115.2 7.3 %select_reduce_fusion = bf16[1024,128]{1,0:T(8,128)(2,1)S(1)} fusion(pred[1024,16]{1,0:T(8,128)(4,1)S(1)} %copy.30, pred[1024,16]{1,0:T(8,128)(4,1)S(1)} %copy.29, bf16[16384,128]{1,0:T(8,128)(2,1)} %gather_fusion), kind=kLoop, calls=%fused_computation.8 | loop fusion | flops 8257536 | bytes 4489216 | tf_op jit(solution)/shard_map/while/body/eval_jaxpr/reduce_sum | solution.py:24
  122.5 10.5 %all_to_all.20 = bf16[1,8,128,128]{3,2,0,1:T(8,128)(2,1)} all-to-all(bf16[1,8,128,128]{3,2,0,1:T(8,128)(2,1)S(1)} %bitcast.82), channel_id=1, replica_groups=mesh['wide'=8,'narrow'=4] {'wide'}, dimensions={1} | all-to-all | bytes 524288 | tf_op jit(solution)/shard_map/all_to_all | solution.py:77
  133.0 0.0 all-gather.7.cloned.1.call-update
  133.0 0.0 reduce-scatter.2.cloned.1.call-start
  133.1 25.1 %all-gather.7.cloned.1.call-done = bf16[1,8,512,128]{3,2,1,0:T(8,128)(2,1)} async-done(((bf16[1,8,128,128]{3,2,1,0:T(8,128)(2,1)}), bf16[1,8,512,128]{3,2,1,0:T(8,128)(2,1)}) %all-gather.7.cloned.1.call-update) | async-done | bytes 1048592 | tf_op jit(solution)/shard_map/all_gather | solution.py:79
  158.1 0.0 copy-done
  158.1 0.0 copy-done.8
  158.1 12.5 %fusion.13 = f32[512,4096]{1,0:T(8,128)} fusion(bf16[1024,4096]{1,0:T(8,128)(2,1)} %param.19, bf16[8,128,1024]{2,1,0:T(8,128)(2,1)S(1)} %bitcast.79, bf16[1,8,512,128]{3,2,1,0:T(8,128)(2,1)} %all-gather.7.cloned.1.call-done, f32[1024]{0:T(1024)S(1)} %copy-done.8), kind=kOutput, calls=%fused_computation.21 | convolution fusion | flops 5370281984 | bytes 19927040 | tf_op jit(solution)/shard_map/dot_general | solution.py:83
  170.7 0.0 reduce-scatter.2.cloned.1.call-update
  170.7 0.6 copy-done.6
  171.3 0.2 reduce-window.8
  171.5 0.1 maximum_bitcast_fusion
  171.6 0.0 copy-done.1
  171.6 0.0 copy-start.7
  171.6 8.6 %gather_fusion.1 = s32[2048]{0:T(1024)S(1)} fusion(s32[1024]{0:T(1024)S(1)} %bitcast.80, s32[2048]{0:T(1024)S(1)} %broadcast_clamp_fusion.2), kind=kCustom, calls=%fused_computation.1 | custom fusion | bytes 24576 | tf_op jit(solution)/shard_map/jit(_take)/gather | solution.py:107
  180.2 0.0 copy-start.5
  180.2 0.0 copy-start.3
  180.2 0.7 compare_select_fusion.3
  180.9 3.2 all-to-all-start.1
  184.2 0.0 copy-done.7
  184.2 2.4 fusion.5
  186.6 0.0 copy-done.5
  186.6 3.3 all-to-all-done.1
  189.9 3.7 %all-to-all-start.2 = ((bf16[4,512,128]{2,1,0:T(8,128)(2,1)}), bf16[4,512,128]{2,1,0:T(8,128)(2,1)S(1)}, u32[]{:S(2)}, u32[]{:S(2)}) async-start(bf16[4,512,128]{2,1,0:T(8,128)(2,1)} %bitcast.18), calls=%async_computation.3 | async-start | bytes 1048576 | tf_op jit(solution)/shard_map/all_to_all | solution.py:111
  193.7 2.1 convert_reduce_fusion
  195.7 26.5 %all-to-all-done.2 = bf16[4,512,128]{2,1,0:T(8,128)(2,1)S(1)} async-done(((bf16[4,512,128]{2,1,0:T(8,128)(2,1)}), bf16[4,512,128]{2,1,0:T(8,128)(2,1)S(1)}, u32[]{:S(2)}, u32[]{:S(2)}) %all-to-all-start.2) | async-done | bytes 524320 | tf_op jit(solution)/shard_map/all_to_all | solution.py:111
  222.2 0.0 copy-done.3
  222.2 5.8 %fusion.8 = bf16[1,2048,128]{2,1,0:T(8,128)(2,1)} fusion(bf16[2048,128]{1,0:T(8,128)(2,1)S(1)} %bitcast.87, s32[2048]{0:T(1024)S(1)} %and_select_fusion, bf16[1,2048,128]{2,1,0:T(8,128)(2,1)S(1)} %copy-done.3, pred[2048]{0:T(1024)(128)(4,1)S(1)} %broadcast_compare_fusion.2), kind=kOutput, calls=%fused_computation.14 | convolution fusion | flops 1078460416 | bytes 1583104 | tf_op jit(solution)/shard_map/as,ae->se/dot_general | solution.py:122
  228.0 95.3 %reduce-scatter.2.cloned.1.call-done = f32[512,1024]{1,0:T(8,128)} async-done(((f32[512,4096]{1,0:T(8,128)}), f32[512,1024]{1,0:T(8,128)}) %reduce-scatter.2.cloned.1.call-update) | async-done | bytes 2097168 | tf_op jit(solution)/shard_map/reduce_scatter | solution.py:84
  323.3 0.0 copy-done.4
  323.3 1.9 maximum_convert_fusion
  325.2 0.0 copy-start.2
  325.2 0.4 fusion.20
  325.6 12.9 %psum.7 = f32[512]{0:T(512)} all-reduce(f32[512]{0:T(512)S(1)} %bitcast.94), channel_id=1, replica_groups=mesh['wide'=8,'narrow'=4] {'narrow'}, use_global_device_ids=true, to_apply=%region_2.3 | all-reduce | flops 512 | bytes 4096 | tf_op jit(solution)/shard_map/psum | solution.py:87
  (20 shorter events, 0.2 us)
Async XLA Ops:
  7.2 151.0 %copy-start = (bf16[1024,1024]{1,0:T(8,128)(2,1)S(1)}, bf16[1024,1024]{1,0:T(8,128)(2,1)}, u32[]{:S(2)}) copy-start(bf16[1024,1024]{1,0:T(8,128)(2,1)} %param.17) | copy-start | bytes 6291460
  7.2 50.8 %all-gather.5.cloned.1.call-start = ((), (), s32[]{:S(2)}) async-start(), calls=%async_computation.5 | async-start | bytes 2621440 | tf_op jit(solution)/shard_map/all_gather | solution.py:60
  7.9 150.2 %all-gather.7.cloned.1.call-start = ((), (), s32[]{:S(2)}) async-start(), calls=%async_computation.6 | async-start | bytes 1310720 | tf_op jit(solution)/shard_map/all_gather | solution.py:79
  115.2 42.9 %copy-start.8 = (f32[1024]{0:T(1024)S(1)}, f32[1024]{0:T(1024)}, u32[]{:S(2)}) copy-start(f32[1024]{0:T(1024)} %param.18) | copy-start | bytes 12292
  133.0 190.3 %reduce-scatter.2.cloned.1.call-start = ((), (), s32[]{:S(2)}) async-start(), calls=%async_computation.4 | async-start | bytes 10485760 | tf_op jit(solution)/shard_map/reduce_scatter | solution.py:84
  170.7 0.7 copy-start.6
  170.7 0.9 copy-start.1
  171.6 12.6 %copy-start.7 = (bf16[1,1024,128]{2,1,0:T(8,128)(2,1)S(1)}, bf16[1,1024,128]{2,1,0:T(8,128)(2,1)}, u32[]{:S(2)}) copy-start(bf16[1,1024,128]{2,1,0:T(8,128)(2,1)} %param.14) | copy-start | bytes 786436
  180.2 6.4 %copy-start.5 = (bf16[1024]{0:T(1024)(128)(2,1)S(1)}, bf16[1024]{0:T(1024)(128)(2,1)}, u32[]{:S(2)}) copy-start(bf16[1024]{0:T(1024)(128)(2,1)} %param.21) | copy-start | bytes 6148
  180.2 42.0 %copy-start.3 = (bf16[1,2048,128]{2,1,0:T(8,128)(2,1)S(1)}, bf16[1,2048,128]{2,1,0:T(8,128)(2,1)}, u32[]{:S(2)}) copy-start(bf16[1,2048,128]{2,1,0:T(8,128)(2,1)} %param.11) | copy-start | bytes 1572868
  180.9 9.0 %all-to-all-start.1 = ((s32[4,1,512]{2,1,0:T(1,128)}), s32[4,1,512]{2,1,0:T(1,128)S(1)}, u32[]{:S(2)}, u32[]{:S(2)}) async-start(s32[4,1,512]{2,1,0:T(1,128)} %compare_select_fusion.3), calls=%async_computation.2 | async-start | bytes 16384 | tf_op jit(solution)/shard_map/all_to_all | solution.py:112
  189.9 32.3 %all-to-all-start.2 = ((bf16[4,512,128]{2,1,0:T(8,128)(2,1)}), bf16[4,512,128]{2,1,0:T(8,128)(2,1)S(1)}, u32[]{:S(2)}, u32[]{:S(2)}) async-start(bf16[4,512,128]{2,1,0:T(8,128)(2,1)} %bitcast.18), calls=%async_computation.3 | async-start | bytes 1048576 | tf_op jit(solution)/shard_map/all_to_all | solution.py:111
  222.2 101.1 %copy-start.4 = (f32[1024]{0:T(1024)S(1)}, f32[1024]{0:T(1024)}, u32[]{:S(2)}) copy-start(f32[1024]{0:T(1024)} %param.20) | copy-start | bytes 12292
  325.2 13.3 %copy-start.2 = (bf16[512,1024]{1,0:T(8,128)(2,1)}, bf16[512,1024]{1,0:T(8,128)(2,1)S(1)}, u32[]{:S(2)}) copy-start(bf16[512,1024]{1,0:T(8,128)(2,1)S(1)} %maximum_convert_fusion) | copy-start | bytes 3145732
Sparse Core Ops, SparseCore 0:
  9.6 48.3 all-gather.4
  133.1 24.9 all-gather.6
  170.8 152.4 reduce-scatter.1
where the time goes:
time: 346 us; the launch traced here: 345 us
  waiting for transfers between devices  198 us (57%)
  local copies, waits for them, and re-layouts  69.3 us (20%)
  blocking collectives  23.4 us (7%)
  matrix products  21.1 us (6%)
  between operations  14 us (4%)
  other arithmetic  12.4 us (4%)
  starting transfers between devices  7.02 us (2%)
    reduce_scatter x1, waiting for transfers between devices, body(): lax.psum_scatter(second_terms, 'narrow', scatter_dimension=1, tiled=True)  95.3 us
    gather x1, local copies, waits for them, and re-layouts, pool_block(): gathered = jnp.take(cache_table, positions, axis=0).astype(jnp.float32)  57.2 us
    all_gather x1, waiting for transfers between devices, body(): whole_table = lax.all_gather(cache_table, 'narrow', axis=0, tiled=True)  46.9 us
    all_to_all x1, waiting for transfers between devices, body(): lax.all_to_all(slab_rows, 'narrow', split_axis=0, concat_axis=0, tiled=True)  26.5 us
    all_gather x1, waiting for transfers between devices, body(): pooled = lax.all_gather(arrived, 'narrow', axis=1, tiled=True)  25.1 us
    psum x1, blocking collectives, body(): logits = lax.psum(logit_terms, 'narrow')  12.9 us
    dot_general x1, matrix products, body(): jnp.dot(first_hidden, w_second, preferred_element_type=jnp.float32)  12.5 us
    all_to_all x1, blocking collectives, body(): lax.all_to_all(summed, 'wide', split_axis=1, concat_axis=0, tiled=True)  10.5 us
  transfers between devices with their start and end apart: 5, of which 5 were waited for; matrix products, arithmetic and copies ran while one was open for 7% of the time, Pallas kernels for 0%

commit v1 on v0

--- a/solution.py
+++ b/solution.py
@@ -5,6 +5,31 @@
 from jax.sharding import PartitionSpec as P
 
 SEND_CAP = 512
+
+
+def in_order(pieces, dim):
+    pieces = jnp.moveaxis(pieces, 0, dim)
+    shape = pieces.shape
+    return pieces.reshape(*shape[:dim], shape[dim] * shape[dim + 1], *shape[dim + 2 :])
+
+
+def ring_apply(shard, axis, dim, apply, out_dim):
+    size, index, rows = (lax.axis_size(axis), lax.axis_index(axis), shard.shape[dim])
+    forward = [(i, (i + 1) % size) for i in range(size)]
+    downward = [(i, (i - 1) % size) for i in range(size)]
+    half = size // 2
+    parts = {}
+    from_left = from_right = shard
+    for step in range(half + 1):
+        next_left = lax.ppermute(from_left, axis, forward) if step < half else None
+        next_right = lax.ppermute(from_right, axis, downward) if step < size - half - 1 else None
+        parts[-step] = apply(from_left, (index - step) % size * rows)
+        if 0 < step < size - half:
+            parts[step] = apply(from_right, (index + step) % size * rows)
+        from_left, from_right = (next_left, next_right)
+    parts = jnp.stack([parts[k] for k in sorted(parts)])
+    parts = parts[(jnp.arange(size) - index + half) % size]
+    return in_order(parts, out_dim)
 
 
 def pool_rows(cache_table, lookups, lengths, owner_index):
@@ -76,9 +101,16 @@
     summed = own_pooled.reshape(1, wide_count, quarter_rows, emb_width).astype(jnp.bfloat16)
     arrived = lax.all_to_all(summed, "wide", split_axis=1, concat_axis=0, tiled=True)
     arrived = arrived.reshape(wide_count, quarter_rows, emb_width)
-    pooled = lax.all_gather(arrived, "narrow", axis=1, tiled=True)
     first_slab = w_first.reshape(wide_count, emb_width, w_first.shape[1])
-    first_terms = jnp.einsum("fbe,feh->bh", pooled, first_slab, preferred_element_type=jnp.float32)
+    first_terms = ring_apply(
+        arrived,
+        "narrow",
+        1,
+        lambda own_block, start: jnp.einsum(
+            "fbe,feh->bh", own_block, first_slab, preferred_element_type=jnp.float32
+        ),
+        0,
+    )
     first_hidden = jnp.maximum(first_terms + b_first, 0.0).astype(jnp.bfloat16)
     second_terms = jnp.dot(first_hidden, w_second, preferred_element_type=jnp.float32)
     second_summed = lax.psum_scatter(second_terms, "narrow", scatter_dimension=1, tiled=True)

time: 346 us -> 345 us (level)
  blocking collectives: 23.4 us -> 12.9 us
  starting transfers between devices: 7.02 us -> 14.5 us
  waiting for transfers between devices: 198 us -> 193 us
  other arithmetic: 12.4 us -> 16.5 us
  local copies, waits for them, and re-layouts: 69.3 us -> 72.9 us
    all_gather x1 -> x0, waiting for transfers between devices: 25.1 us -> none  [body(): pooled = lax.all_gather(arrived, 'narrow', axis=1, tiled=True)]
    ppermute x0 -> x3, waiting for transfers between devices: none -> 15.4 us  [the longest x2 13.7 us: ring_apply(): next_left = lax.ppermute(from_left, axis, forward) if step < half else None]
    all_to_all x1 -> x0, blocking collectives: 10.5 us -> none  [body(): lax.all_to_all(summed, 'wide', split_axis=1, concat_axis=0, tiled=True)]
    all_to_all x0 -> x1, waiting for transfers between devices: none -> 6.83 us  [body(): lax.all_to_all(summed, 'wide', split_axis=1, concat_axis=0, tiled=True)]
    ppermute x0 -> x3, starting transfers between devices: none -> 3.83 us  [the longest x1 3.64 us: ring_apply(): lax.ppermute(from_right, axis, downward)]
    all_to_all x0 -> x1, starting transfers between devices: none -> 3.66 us  [body(): lax.all_to_all(summed, 'wide', split_axis=1, concat_axis=0, tiled=True)]
    gather x0 -> x1, local copies, waits for them, and re-layouts: none -> 3.59 us  [ring_apply(): parts = parts[(jnp.arange(size) - index + half) % size]]
  transfers between devices with their start and end apart: 5 -> 8, of which waited for: 5 -> 8; matrix products, arithmetic and copies ran while one was open for 7% -> 7% of each run, Pallas kernels for 0% -> 0%
where the time goes in v1:
time: 345 us; the launch traced here: 344 us
  waiting for transfers between devices  193 us (56%)
  local copies, waits for them, and re-layouts  72.9 us (21%)
  matrix products  20.5 us (6%)
  other arithmetic  16.5 us (5%)
  starting transfers between devices  14.5 us (4%)
  between operations  14.3 us (4%)
  blocking collectives  12.9 us (4%)
    reduce_scatter x1, waiting for transfers between devices, body(): lax.psum_scatter(second_terms, 'narrow', scatter_dimension=1, tiled=True)  94.8 us
    gather x1, local copies, waits for them, and re-layouts, pool_block(): gathered = jnp.take(cache_table, positions, axis=0).astype(jnp.float32)  57.2 us
    all_gather x1, waiting for transfers between devices, body(): whole_table = lax.all_gather(cache_table, 'narrow', axis=0, tiled=True)  47 us
    all_to_all x1, waiting for transfers between devices, body(): lax.all_to_all(slab_rows, 'narrow', split_axis=0, concat_axis=0, tiled=True)  24.5 us
    ppermute x2, waiting for transfers between devices, ring_apply(): next_left = lax.ppermute(from_left, axis, forward) if step < half else None  13.7 us
    psum x1, blocking collectives, body(): logits = lax.psum(logit_terms, 'narrow')  12.9 us
    dot_general x1, matrix products, body(): jnp.dot(first_hidden, w_second, preferred_element_type=jnp.float32)  10.1 us
    gather x1, local copies, waits for them, and re-layouts, body(): jnp.take(sectioned_slots, jnp.maximum(sources, 0), axis=0)  8.58 us
  transfers between devices with their start and end apart: 8, of which 8 were waited for; matrix products, arithmetic and copies ran while one was open for 7% of the time, Pallas kernels for 0%

profile of v1, /device:TPU:0, one launch (start us, length us, event | category | flops | bytes accessed | tf_op | source)
XLA Modules:
  0.0 344.1 jit_solution(5003428674383776828)
XLA Ops:
  7.2 0.0 copy-start
  7.2 0.0 all-gather.3.cloned.1.call-start
  7.2 0.7 all-gather.3.cloned.1.call-update
  7.9 1.1 reshape_squeeze.7
  9.1 0.7 constant_dynamic-slice_fusion.1
  9.8 0.1 constant_dynamic-slice_fusion
  9.9 0.3 copy.28
  10.2 0.2 copy.30
  10.4 0.1 compare_select_fusion
  10.5 0.2 reshape.401
  10.7 0.3 copy.29
  11.0 47.0 %all-gather.3.cloned.1.call-done = bf16[1,8192,128]{2,1,0:T(8,128)(2,1)} async-done(((bf16[1,2048,128]{2,1,0:T(8,128)(2,1)}), bf16[1,8192,128]{2,1,0:T(8,128)(2,1)}) %all-gather.3.cloned.1.call-update) | async-done | bytes 2097168 | tf_op jit(solution)/shard_map/all_gather | solution.py:85
  58.0 57.2 %gather_fusion = bf16[16384,128]{1,0:T(8,128)(2,1)} fusion(bf16[8192,128]{1,0:T(8,128)(2,1)} %bitcast.100, s32[16384]{0:T(1024)S(1)} %broadcast_clamp_fusion), kind=kCustom, calls=%fused_computation | custom fusion | bytes 8454144 | tf_op jit(solution)/shard_map/while/body/eval_jaxpr/jit(_take)/gather | solution.py:48
  115.2 8.0 %select_reduce_fusion = bf16[1024,128]{1,0:T(8,128)(2,1)} fusion(pred[1024,16]{1,0:T(8,128)(4,1)S(1)} %copy.29, pred[1024,16]{1,0:T(8,128)(4,1)S(1)} %copy.28, bf16[16384,128]{1,0:T(8,128)(2,1)} %gather_fusion), kind=kLoop, calls=%fused_computation.9 | loop fusion | flops 8257536 | bytes 4489216 | tf_op jit(solution)/shard_map/while/body/eval_jaxpr/reduce_sum | solution.py:49
  123.2 3.7 %all-to-all-start = ((bf16[1,8,128,128]{3,2,0,1:T(8,128)(2,1)}), bf16[1,8,128,128]{3,2,0,1:T(8,128)(2,1)S(1)}, u32[]{:S(2)}, u32[]{:S(2)}) async-start(bf16[1,8,128,128]{3,2,0,1:T(8,128)(2,1)} %bitcast.5), calls=%async_computation | async-start | bytes 524288 | tf_op jit(solution)/shard_map/all_to_all | solution.py:102
  126.9 0.0 reduce-scatter.2.cloned.1.call-start
  126.9 6.8 %all-to-all-done = bf16[1,8,128,128]{3,2,0,1:T(8,128)(2,1)S(1)} async-done(((bf16[1,8,128,128]{3,2,0,1:T(8,128)(2,1)}), bf16[1,8,128,128]{3,2,0,1:T(8,128)(2,1)S(1)}, u32[]{:S(2)}, u32[]{:S(2)}) %all-to-all-start) | async-done | bytes 262176 | tf_op jit(solution)/shard_map/all_to_all | solution.py:102
  133.8 0.2 collective-permute-start
  133.9 3.6 %collective-permute-start.2 = (bf16[8,128,128]{2,1,0:T(8,128)(2,1)S(1)}, bf16[8,128,128]{2,1,0:T(8,128)(2,1)S(1)}, u32[]{:S(2)}, u32[]{:S(2)}) collective-permute-start(bf16[8,128,128]{2,1,0:T(8,128)(2,1)S(1)} %bitcast.102), channel_id=1, source_target_pairs={{0,3},{1,0},{2,1},{3,2},{4,7},{5,4},{6,5},{7,6},{8,11},{9,8},{10,9... | collective-permute-start | bytes 786440 | tf_op jit(solution)/shard_map/ppermute | solution.py:25
  137.6 0.4 convolution_bitcast_fusion.1
  138.0 6.7 %collective-permute-done = bf16[8,128,128]{2,1,0:T(8,128)(2,1)S(1)} collective-permute-done((bf16[8,128,128]{2,1,0:T(8,128)(2,1)S(1)}, bf16[8,128,128]{2,1,0:T(8,128)(2,1)S(1)}, u32[]{:S(2)}, u32[]{:S(2)}) %collective-permute-start) | collective-permute-done | bytes 262176 | tf_op jit(solution)/shard_map/ppermute | solution.py:24
  144.8 0.4 convolution_bitcast_fusion.2
  145.2 1.7 collective-permute-done.2
  146.9 0.4 convolution_bitcast_fusion
  147.3 7.0 %collective-permute-done.1 = bf16[8,128,128]{2,1,0:T(8,128)(2,1)S(1)} collective-permute-done((bf16[8,128,128]{2,1,0:T(8,128)(2,1)S(1)}, bf16[8,128,128]{2,1,0:T(8,128)(2,1)S(1)}, u32[]{:S(2)}, u32[]{:S(2)}) %collective-permute-start.1) | collective-permute-done | bytes 262176 | tf_op jit(solution)/shard_map/ppermute | solution.py:24
  154.3 0.4 convolution_bitcast_fusion.3
  154.8 1.5 pad_maximum_fusion
  156.3 3.6 %gather_fusion.1 = f32[4,128,1024]{2,1,0:T(8,128)} fusion(f32[4,128,1024]{2,1,0:T(8,128)} %pad_maximum_fusion, s32[1024]{0:T(1024)S(1)} %pad_clamp_fusion), kind=kCustom, calls=%fused_computation.1 | custom fusion | bytes 4194320 | tf_op jit(solution)/shard_map/gather | solution.py:31
  159.9 1.9 fusion.10
  161.7 10.1 %fusion.18 = f32[512,4096]{1,0:T(8,128)} fusion(bf16[512,1024]{1,0:T(8,128)(2,1)S(1)} %fusion.10, bf16[1024,4096]{1,0:T(8,128)(2,1)} %param.19), kind=kOutput, calls=%fused_computation.59 | convolution fusion | flops 4294967296 | bytes 17825792 | tf_op jit(solution)/shard_map/dot_general | solution.py:115
  171.8 0.0 reduce-scatter.2.cloned.1.call-update
  171.9 0.6 copy-done.7
  172.5 0.2 reduce-window.8
  172.7 0.1 maximum_bitcast_fusion
  172.8 0.0 copy-start.8
  172.8 8.6 %gather_fusion.2 = s32[2048]{0:T(1024)S(1)} fusion(s32[1024]{0:T(1024)S(1)} %bitcast.99, s32[2048]{0:T(1024)S(1)} %broadcast_clamp_fusion.2), kind=kCustom, calls=%fused_computation.2 | custom fusion | bytes 24576 | tf_op jit(solution)/shard_map/jit(_take)/gather | solution.py:139
  181.4 0.7 compare_select_fusion.3
  182.1 3.3 all-to-all-start.1
  185.4 2.4 fusion.5
  187.8 3.4 all-to-all-done.1
  191.2 3.7 %all-to-all-start.2 = ((bf16[4,512,128]{2,1,0:T(8,128)(2,1)}), bf16[4,512,128]{2,1,0:T(8,128)(2,1)S(1)}, u32[]{:S(2)}, u32[]{:S(2)}) async-start(bf16[4,512,128]{2,1,0:T(8,128)(2,1)} %bitcast.26), calls=%async_computation.3 | async-start | bytes 1048576 | tf_op jit(solution)/shard_map/all_to_all | solution.py:143
  194.9 2.1 convert_reduce_fusion
  197.0 24.5 %all-to-all-done.2 = bf16[4,512,128]{2,1,0:T(8,128)(2,1)S(1)} async-done(((bf16[4,512,128]{2,1,0:T(8,128)(2,1)}), bf16[4,512,128]{2,1,0:T(8,128)(2,1)S(1)}, u32[]{:S(2)}, u32[]{:S(2)}) %all-to-all-start.2) | async-done | bytes 524320 | tf_op jit(solution)/shard_map/all_to_all | solution.py:143
  221.5 5.8 %fusion.8 = bf16[1,2048,128]{2,1,0:T(8,128)(2,1)} fusion(bf16[2048,128]{1,0:T(8,128)(2,1)S(1)} %bitcast.106, s32[2048]{0:T(1024)S(1)} %and_select_fusion, bf16[1,2048,128]{2,1,0:T(8,128)(2,1)S(1)} %copy-done.3, pred[2048]{0:T(1024)(128)(4,1)S(1)} %broadcast_compare_fusion.2), kind=kOutput, calls=%fused_computation.15 | convolution fusion | flops 1078460416 | bytes 1583104 | tf_op jit(solution)/shard_map/as,ae->se/dot_general | solution.py:154
  227.3 94.8 %reduce-scatter.2.cloned.1.call-done = f32[512,1024]{1,0:T(8,128)} async-done(((f32[512,4096]{1,0:T(8,128)}), f32[512,1024]{1,0:T(8,128)}) %reduce-scatter.2.cloned.1.call-update) | async-done | bytes 2097168 | tf_op jit(solution)/shard_map/reduce_scatter | solution.py:116
  322.1 1.9 maximum_convert_fusion
  323.9 0.4 fusion.19
  324.3 12.9 %psum.7 = f32[512]{0:T(512)} all-reduce(f32[512]{0:T(512)S(1)} %bitcast.113), channel_id=1, replica_groups=mesh['wide'=8,'narrow'=4] {'narrow'}, use_global_device_ids=true, to_apply=%region_2.3 | all-reduce | flops 512 | bytes 4096 | tf_op jit(solution)/shard_map/psum | solution.py:119
  (33 shorter events, 0.3 us)
Async XLA Ops:
  7.2 130.4 %copy-start = (bf16[1024,1024]{1,0:T(8,128)(2,1)S(1)}, bf16[1024,1024]{1,0:T(8,128)(2,1)}, u32[]{:S(2)}) copy-start(bf16[1024,1024]{1,0:T(8,128)(2,1)} %param.17) | copy-start | bytes 6291460
  7.2 50.8 %all-gather.3.cloned.1.call-start = ((), (), s32[]{:S(2)}) async-start(), calls=%async_computation.5 | async-start | bytes 2621440 | tf_op jit(solution)/shard_map/all_gather | solution.py:85
  123.2 10.6 %all-to-all-start = ((bf16[1,8,128,128]{3,2,0,1:T(8,128)(2,1)}), bf16[1,8,128,128]{3,2,0,1:T(8,128)(2,1)S(1)}, u32[]{:S(2)}, u32[]{:S(2)}) async-start(bf16[1,8,128,128]{3,2,0,1:T(8,128)(2,1)} %bitcast.5), calls=%async_computation | async-start | bytes 524288 | tf_op jit(solution)/shard_map/all_to_all | solution.py:102
  126.9 195.2 %reduce-scatter.2.cloned.1.call-start = ((), (), s32[]{:S(2)}) async-start(), calls=%async_computation.4 | async-start | bytes 10485760 | tf_op jit(solution)/shard_map/reduce_scatter | solution.py:116
  133.8 11.0 %collective-permute-start = (bf16[8,128,128]{2,1,0:T(8,128)(2,1)S(1)}, bf16[8,128,128]{2,1,0:T(8,128)(2,1)S(1)}, u32[]{:S(2)}, u32[]{:S(2)}) collective-permute-start(bf16[8,128,128]{2,1,0:T(8,128)(2,1)S(1)} %bitcast.101), channel_id=1, source_target_pairs={{0,1},{1,2},{2,3},{3,0},{4,5},{5,6},{6,7},{7,4},{8,9},{9,10},{10,1... | collective-permute-start | bytes 786440 | tf_op jit(solution)/shard_map/ppermute | solution.py:24
  133.9 12.9 %collective-permute-start.2 = (bf16[8,128,128]{2,1,0:T(8,128)(2,1)S(1)}, bf16[8,128,128]{2,1,0:T(8,128)(2,1)S(1)}, u32[]{:S(2)}, u32[]{:S(2)}) collective-permute-start(bf16[8,128,128]{2,1,0:T(8,128)(2,1)S(1)} %bitcast.102), channel_id=1, source_target_pairs={{0,3},{1,0},{2,1},{3,2},{4,7},{5,4},{6,5},{7,6},{8,11},{9,8},{10,9... | collective-permute-start | bytes 786440 | tf_op jit(solution)/shard_map/ppermute | solution.py:25
  144.7 9.6 %collective-permute-start.1 = (bf16[8,128,128]{2,1,0:T(8,128)(2,1)S(1)}, bf16[8,128,128]{2,1,0:T(8,128)(2,1)S(1)}, u32[]{:S(2)}, u32[]{:S(2)}) collective-permute-start(bf16[8,128,128]{2,1,0:T(8,128)(2,1)S(1)} %collective-permute-done), channel_id=1, source_target_pairs={{0,1},{1,2},{2,3},{3,0},{4,5},{5,6},{6,7},{7,4},{8,9},{9,10},{10,1... | collective-permute-start | bytes 786440 | tf_op jit(solution)/shard_map/ppermute | solution.py:24
  156.3 3.6 %copy-start.4 = (f32[1024]{0:T(1024)S(1)}, f32[1024]{0:T(1024)}, u32[]{:S(2)}) copy-start(f32[1024]{0:T(1024)} %param.18) | copy-start | bytes 12292
  171.8 0.7 copy-start.7
  171.9 0.9 copy-start.1
  172.8 12.6 %copy-start.8 = (bf16[1,1024,128]{2,1,0:T(8,128)(2,1)S(1)}, bf16[1,1024,128]{2,1,0:T(8,128)(2,1)}, u32[]{:S(2)}) copy-start(bf16[1,1024,128]{2,1,0:T(8,128)(2,1)} %param.14) | copy-start | bytes 786436
  182.1 9.1 %all-to-all-start.1 = ((s32[4,1,512]{2,1,0:T(1,128)}), s32[4,1,512]{2,1,0:T(1,128)S(1)}, u32[]{:S(2)}, u32[]{:S(2)}) async-start(s32[4,1,512]{2,1,0:T(1,128)} %compare_select_fusion.3), calls=%async_computation.2 | async-start | bytes 16384 | tf_op jit(solution)/shard_map/all_to_all | solution.py:144
  185.4 2.4 copy-start.6
  185.4 36.1 %copy-start.3 = (bf16[1,2048,128]{2,1,0:T(8,128)(2,1)S(1)}, bf16[1,2048,128]{2,1,0:T(8,128)(2,1)}, u32[]{:S(2)}) copy-start(bf16[1,2048,128]{2,1,0:T(8,128)(2,1)} %param.11) | copy-start | bytes 1572868
  191.2 30.3 %all-to-all-start.2 = ((bf16[4,512,128]{2,1,0:T(8,128)(2,1)}), bf16[4,512,128]{2,1,0:T(8,128)(2,1)S(1)}, u32[]{:S(2)}, u32[]{:S(2)}) async-start(bf16[4,512,128]{2,1,0:T(8,128)(2,1)} %bitcast.26), calls=%async_computation.3 | async-start | bytes 1048576 | tf_op jit(solution)/shard_map/all_to_all | solution.py:143
  221.5 100.6 %copy-start.5 = (f32[1024]{0:T(1024)S(1)}, f32[1024]{0:T(1024)}, u32[]{:S(2)}) copy-start(f32[1024]{0:T(1024)} %param.20) | copy-start | bytes 12292
  323.9 13.3 %copy-start.2 = (bf16[512,1024]{1,0:T(8,128)(2,1)}, bf16[512,1024]{1,0:T(8,128)(2,1)S(1)}, u32[]{:S(2)}) copy-start(bf16[512,1024]{1,0:T(8,128)(2,1)S(1)} %maximum_convert_fusion) | copy-start | bytes 3145732
Sparse Core Ops, SparseCore 0:
  9.6 48.3 all-gather.2
  172.0 150.0 reduce-scatter.1
